TPU v7x, 32 devices: a whole 2x2x4 slice. The times are simulated.
32 devices in a mesh: ctx: 2 (over x), tok: 8 (over z, core), head: 2 (over y).
Axes of the slice: x: 2, y: 2, z: 4, core: 2. Of those that a mesh axis runs over, the one named last changes fastest.
Arguments:
- keys: bfloat16 [2, 2, 4, 6144, 256], P(None, 'ctx', 'head', 'tok'), may hold values from -6 to 6
- values: bfloat16 [2, 2, 4, 6144, 256], P(None, 'ctx', 'head', 'tok'), may hold values from -6 to 6
- queries: bfloat16 [2, 2, 4, 6144, 256], P(None, 'ctx', 'head', 'tok'), may hold values from -6 to 6
- rates: float32 [2, 2, 4, 6144], P(None, 'ctx', 'head', 'tok'), may hold values from 0.1 to 3, as said below
- state_in: bfloat16 [2, 4, 3, 256, 512], P('ctx', 'head'), may hold values from -0.375 to 0.375
- fresh: bfloat16 [4, 3, 256, 512], P('head'), may hold values from -0.375 to 0.375
Outputs:
- outputs: bfloat16 [2, 2, 4, 6144, 256], P(None, 'ctx', 'head', 'tok')
Inputs may be any that keep to these rules, and one draw needn't show every extreme that they name: Positive per-token learning rates.
All inputs are finite; a program needn't handle non-finite values.
Results may differ from a plain program's by a relative error of at most 0.023.
Values may be sent and summed in bfloat16 or wider, within the bound.
No kernel may reach another device: no remote copies, remote signals or barrier semaphores. Data moves between devices by JAX's collectives and lax.ppermute only.
A program may use at most 64 MiB of HBM per device.

v0:
```python
import jax
import jax.numpy as jnp
from jax import lax
from jax.sharding import PartitionSpec as P


def from_behind(value, axis, steps):
    count = lax.axis_size(axis)
    first, last = (max(0, -steps), min(count, count - steps))
    return lax.ppermute(value, axis, [(source, source + steps) for source in range(first, last)])


def partial_grads(state, keys_p, values_p, rate_p):
    h_one = jnp.dot(keys_p, state[0], preferred_element_type=jnp.float32)
    h_three = jnp.dot(keys_p, state[1], preferred_element_type=jnp.float32)
    sig = jax.nn.sigmoid(h_one)
    act = (h_one * sig * h_three).astype(jnp.bfloat16)
    weighted = (rate_p[:, None] * values_p.astype(jnp.float32)).astype(jnp.bfloat16)
    dact = -jnp.dot(weighted, state[2], preferred_element_type=jnp.float32)
    d_one = (dact * h_three * sig * (1.0 + h_one * (1.0 - sig))).astype(jnp.bfloat16)
    d_three = (dact * h_one * sig).astype(jnp.bfloat16)
    contract = (((0,), (0,)), ((), ()))
    g_one = lax.dot_general(keys_p, d_one, contract, preferred_element_type=jnp.float32)
    g_three = lax.dot_general(keys_p, d_three, contract, preferred_element_type=jnp.float32)
    g_back = -lax.dot_general(weighted, act, contract, preferred_element_type=jnp.float32)
    return jnp.stack([g_one, g_three, g_back])


def apply_state(state, queries_h):
    p_one = jnp.dot(queries_h, state[0], preferred_element_type=jnp.float32)
    p_three = jnp.dot(queries_h, state[1], preferred_element_type=jnp.float32)
    mixed = (jax.nn.silu(p_one) * p_three).astype(jnp.bfloat16)
    contract = (((1,), (1,)), ((), ()))
    return lax.dot_general(mixed, state[2], contract, preferred_element_type=jnp.float32).astype(
        jnp.bfloat16
    )


def renormed(older_bf, grads, total_sq, heads_all, hidden):
    scale = 0.5 * jnp.sqrt(jnp.float32(3 * hidden * heads_all)) / jnp.sqrt(total_sq + 1e-06)
    older = older_bf.astype(jnp.float32)
    moved = older - scale * grads
    old_norm = jnp.sqrt(jnp.sum(older * older, axis=-2, keepdims=True))
    new_norm = jnp.sqrt(jnp.sum(moved * moved, axis=-2, keepdims=True) + 1e-06)
    return (moved * old_norm / new_norm).astype(jnp.bfloat16)


def block_tick(state, keys_t, values_t, rates_t, queries_t):
    heads_all = lax.axis_size("head") * state.shape[0]
    hidden = state.shape[3]
    grads = jax.vmap(partial_grads)(state, keys_t, values_t, rates_t)
    summed = lax.psum(grads.astype(jnp.bfloat16), "tok").astype(jnp.float32)
    total_sq = lax.psum(jnp.sum(summed * summed), "head")
    newer = renormed(state, summed, total_sq, heads_all, hidden)
    applied = jax.vmap(apply_state)(newer, queries_t)
    return (newer, applied)


def shards(keys, values, queries, rates, state_in, fresh):
    first_state, first_out = block_tick(
        state_in[0], keys[0, 0], values[0, 0], rates[0, 0], queries[0, 0]
    )
    arrived = from_behind(first_state, "ctx", 1)
    incoming = jnp.where(lax.axis_index("ctx") == 0, fresh, arrived)
    second_state, second_out = block_tick(
        incoming, keys[1, 0], values[1, 0], rates[1, 0], queries[1, 0]
    )
    return jnp.stack([first_out, second_out])[:, None]


def solution(mesh):
    in_specs = (
        P(None, "ctx", "head", "tok", None),
        P(None, "ctx", "head", "tok", None),
        P(None, "ctx", "head", "tok", None),
        P(None, "ctx", "head", "tok"),
        P("ctx", "head", None, None, None),
        P("head", None, None, None),
    )
    out_specs = P(None, "ctx", "head", "tok", None)
    return jax.shard_map(shards, mesh=mesh, in_specs=in_specs, out_specs=out_specs, check_vma=False)
```

profile of v0, /device:TPU:0, one launch (start us, length us, event | category | flops | bytes accessed | tf_op | source)
XLA Modules:
  0.0 232.4 jit_solution(3632334294932788770)
XLA Ops:
  6.5 1.6 copy.54
  11.0 1.4 fusion.63
  12.5 1.6 fusion.52
  14.0 1.2 fusion.56
  15.3 1.3 maximum_bitcast_fusion
  16.6 64.7 %all-reduce.3.cloned.1.call-done = bf16[2,3,256,512]{3,2,0,1:T(8,128)(2,1)} async-done(((bf16[2,3,256,512]{3,2,0,1:T(8,128)(2,1)}), bf16[2,3,256,512]{3,2,0,1:T(8,128)(2,1)}) %all-reduce.3.cloned.1.call-update) | async-done | bytes 1572880 | tf_op jit(solution)/shard_map/psum | solution.py:52
  81.3 2.9 %fusion.1 = f32[]{:T(128)} fusion(bf16[2,3,256,512]{3,2,0,1:T(8,128)(2,1)} %all-reduce.3.cloned.1.call-done), kind=kLoop, calls=%fused_computation.9 | loop fusion | flops 2359295 | bytes 1572868 | tf_op jit(solution)/shard_map/reduce_sum | solution.py:53
  84.2 5.5 %psum.29 = f32[]{:T(128)} all-reduce(f32[]{:T(128)} %fusion.1), channel_id=1, replica_groups=mesh['ctx'=2,'tok'=8,'head'=2] {'head'}, use_global_device_ids=true, to_apply=%region_2.0 | all-reduce | flops 1 | bytes 8 | tf_op jit(solution)/shard_map/psum | solution.py:53
  90.5 2.3 fusion
  92.8 1.8 divide_convert_fusion.1
  94.7 4.6 %collective-permute-start = (bf16[2,3,256,512]{3,2,0,1:T(8,128)(2,1)}, bf16[2,3,256,512]{3,2,0,1:T(8,128)(2,1)}, u32[]{:S(2)}, u32[]{:S(2)}) collective-permute-start(bf16[2,3,256,512]{3,2,0,1:T(8,128)(2,1)} %divide_convert_fusion.1), channel_id=1, source_target_pairs={{0,16},{1,17},{2,18},{3,19},{4,20},{5,21},{6,22},{7,23},{8,24},{9,... | collective-permute-start | bytes 4718600 | tf_op jit(solution)/shard_map/ppermute | solution.py:10
  99.3 30.1 %collective-permute-done = bf16[2,3,256,512]{3,2,0,1:T(8,128)(2,1)} collective-permute-done((bf16[2,3,256,512]{3,2,0,1:T(8,128)(2,1)}, bf16[2,3,256,512]{3,2,0,1:T(8,128)(2,1)}, u32[]{:S(2)}, u32[]{:S(2)}) %collective-permute-start) | collective-permute-done | bytes 1572896 | tf_op jit(solution)/shard_map/ppermute | solution.py:10
  129.4 1.6 copy_select_fusion
  133.6 1.4 fusion.60
  135.1 1.5 fusion.53
  136.6 1.2 fusion.57
  137.8 1.3 maximum_bitcast_fusion.1
  139.8 3.3 %fusion.74 = f32[2,512,768]{1,2,0:T(8,128)} fusion(bf16[2,1,2,768,256]{4,3,2,1,0:T(8,128)(2,1)S(1)} %copy-done.8, bf16[2,3,256,512]{3,2,0,1:T(8,128)(2,1)} %divide_convert_fusion.1), kind=kOutput, calls=%fused_computation.92 | convolution fusion | flops 402653184 | bytes 4456448 | tf_op jit(solution)/shard_map/vmap()/dot_general | solution.py:30
  143.1 59.2 %all-reduce.5.cloned.1.call-done = bf16[2,3,256,512]{3,2,0,1:T(8,128)(2,1)} async-done(((bf16[2,3,256,512]{3,2,0,1:T(8,128)(2,1)}), bf16[2,3,256,512]{3,2,0,1:T(8,128)(2,1)}) %all-reduce.5.cloned.1.call-update) | async-done | bytes 1572880 | tf_op jit(solution)/shard_map/psum | solution.py:52
  202.2 2.8 %fusion.3 = f32[]{:T(128)} fusion(bf16[2,3,256,512]{3,2,0,1:T(8,128)(2,1)} %all-reduce.5.cloned.1.call-done), kind=kLoop, calls=%fused_computation.11 | loop fusion | flops 2359295 | bytes 1572868 | tf_op jit(solution)/shard_map/reduce_sum | solution.py:53
  205.0 4.7 %fusion.46 = bf16[1,2,768,256]{3,2,1,0:T(8,128)(2,1)} fusion(f32[2,512,768]{1,2,0:T(8,128)} %fusion.74, bf16[2,1,2,768,256]{4,3,2,1,0:T(8,128)(2,1)} %param.8, bf16[2,3,256,512]{3,2,0,1:T(8,128)(2,1)} %divide_convert_fusion.1), kind=kOutput, calls=%fused_computation.73 | convolution fusion | flops 810418176 | bytes 5767168 | tf_op jit(solution)/shard_map/vmap()/dot_general | solution.py:34
  209.7 5.5 %psum.31 = f32[]{:T(128)} all-reduce(f32[]{:T(128)} %fusion.3), channel_id=1, replica_groups=mesh['ctx'=2,'tok'=8,'head'=2] {'head'}, use_global_device_ids=true, to_apply=%region_7.8 | all-reduce | flops 1 | bytes 8 | tf_op jit(solution)/shard_map/psum | solution.py:53
  219.3 3.6 %fusion.47 = bf16[1,2,768,256]{3,2,1,0:T(8,128)(2,1)} fusion(f32[2,512,768]{1,2,0:T(8,128)S(1)} %fusion.64, bf16[2,1,2,768,256]{4,3,2,1,0:T(8,128)(2,1)} %param.8, bf16[2,3,256,512]{3,2,0,1:T(8,128)(2,1)} %copy-done.5), kind=kOutput, calls=%fused_computation.74 | convolution fusion | flops 810418176 | bytes 5767168 | tf_op jit(solution)/shard_map/vmap()/dot_general | solution.py:34
  222.9 2.7 %maximum_bitcast_fusion.2 = bf16[2,1,2,768,256]{4,3,2,1,0:T(8,128)(2,1)} fusion(bf16[1,2,768,256]{3,2,1,0:T(8,128)(2,1)} %fusion.47, bf16[1,2,768,256]{3,2,1,0:T(8,128)(2,1)} %fusion.46), kind=kLoop, calls=%fused_computation.52 | loop fusion | flops 786432 | bytes 3145728 | tf_op jit(solution)/shard_map/broadcast_in_dim | solution.py:68
  (40 shorter events, 9.5 us)
Async XLA Ops:
  6.5 1.9 copy-start.3
  6.5 74.8 %all-reduce.3.cloned.1.call-start = ((), (), s32[]{:S(2)}) async-start(), calls=%async_computation | async-start | bytes 3145728 | tf_op jit(solution)/shard_map/psum | solution.py:52
  9.0 0.7 copy-start.10
  9.0 1.4 copy-start.6
  15.2 75.2 %copy-start = (bf16[1,2,3,256,512]{4,3,2,1,0:T(8,128)(2,1)S(1)}, bf16[1,2,3,256,512]{4,3,2,1,0:T(8,128)(2,1)}, u32[]{:S(2)}) copy-start(bf16[1,2,3,256,512]{4,3,2,1,0:T(8,128)(2,1)} %param.10) | copy-start | bytes 4718596
  16.6 185.7 %all-reduce.5.cloned.1.call-start = ((), (), s32[]{:S(2)}) async-start(), calls=%async_computation.1 | async-start | bytes 3145728 | tf_op jit(solution)/shard_map/psum | solution.py:52
  81.3 11.5 %copy-start.2 = (bf16[2,3,256,512]{3,2,0,1:T(8,128)(2,1)S(1)}, bf16[2,3,256,512]{3,2,0,1:T(8,128)(2,1)}, u32[]{:S(2)}) copy-start(bf16[2,3,256,512]{3,2,0,1:T(8,128)(2,1)} %all-reduce.3.cloned.1.call-done) | copy-start | bytes 4718596
  94.7 36.4 %copy-start.4 = (bf16[2,1,2,768,256]{4,3,2,1,0:T(8,128)(2,1)S(1)}, bf16[2,1,2,768,256]{4,3,2,1,0:T(8,128)(2,1)}, u32[]{:S(2)}) copy-start(bf16[2,1,2,768,256]{4,3,2,1,0:T(8,128)(2,1)} %param.6) | copy-start | bytes 4718596
  94.7 34.8 %collective-permute-start = (bf16[2,3,256,512]{3,2,0,1:T(8,128)(2,1)}, bf16[2,3,256,512]{3,2,0,1:T(8,128)(2,1)}, u32[]{:S(2)}, u32[]{:S(2)}) collective-permute-start(bf16[2,3,256,512]{3,2,0,1:T(8,128)(2,1)} %divide_convert_fusion.1), channel_id=1, source_target_pairs={{0,16},{1,17},{2,18},{3,19},{4,20},{5,21},{6,22},{7,23},{8,24},{9,... | collective-permute-start | bytes 4718600 | tf_op jit(solution)/shard_map/ppermute | solution.py:10
  131.6 1.4 copy-start.7
  137.8 2.0 copy-start.8
  205.0 10.9 %copy-start.1 = (bf16[2,3,256,512]{3,2,0,1:T(8,128)(2,1)S(1)}, bf16[2,3,256,512]{3,2,0,1:T(8,128)(2,1)}, u32[]{:S(2)}) copy-start(bf16[2,3,256,512]{3,2,0,1:T(8,128)(2,1)} %all-reduce.5.cloned.1.call-done) | copy-start | bytes 4718596
  216.9 1.9 copy-start.9
  217.6 1.1 copy-start.5
Sparse Core Ops, SparseCore 0:
  16.7 64.5 all-reduce.2
  139.3 62.8 all-reduce.4
where the time goes:
time: 233 us; the launch traced here: 232 us
  waiting for transfers between devices  154 us (66%)
  matrix products  24.1 us (10%)
  other arithmetic  18.3 us (8%)
  between operations  15 us (6%)
  blocking collectives  11.1 us (5%)
  local copies, waits for them, and re-layouts  5.34 us (2%)
  starting transfers between devices  4.68 us (2%)
    psum x2, waiting for transfers between devices, block_tick(): summed = lax.psum(grads.astype(jnp.bfloat16), 'tok').astype(jnp.float32)  124 us
    ppermute x1, waiting for transfers between devices, from_behind(): lax.ppermute(value, axis, [(source, source + steps) for source in range(f...  30.1 us
    psum x2, blocking collectives, block_tick(): total_sq = lax.psum(jnp.sum(summed * summed), 'head')  11.1 us
    dot_general x2, matrix products, apply_state(): lax.dot_general(mixed, state[2], contract, preferred_element_type=jnp.flo...  8.33 us
    reduce_sum x2, other arithmetic, block_tick(): total_sq = lax.psum(jnp.sum(summed * summed), 'head')  5.73 us
    unnamed x23, local copies, waits for them, and re-layouts  5.3 us
  transfers between devices with their start and end apart: 3, of which 3 were waited for; matrix products, arithmetic and copies ran while one was open for 1% of the time, Pallas kernels for 0%

commit v1 on v0

--- a/solution.py
+++ b/solution.py
@@ -49,7 +49,7 @@
     heads_all = lax.axis_size("head") * state.shape[0]
     hidden = state.shape[3]
     grads = jax.vmap(partial_grads)(state, keys_t, values_t, rates_t)
-    summed = lax.psum(grads.astype(jnp.bfloat16), "tok").astype(jnp.float32)
+    summed = jnp.sum(lax.all_gather(grads.astype(jnp.bfloat16), "tok"), axis=0).astype(jnp.float32)
     total_sq = lax.psum(jnp.sum(summed * summed), "head")
     newer = renormed(state, summed, total_sq, heads_all, hidden)
     applied = jax.vmap(apply_state)(newer, queries_t)

time: 233 us -> 359 us (1.54)
  waiting for transfers between devices: 154 us -> 264 us
  other arithmetic: 18.3 us -> 30.2 us
    all_gather x0 -> x2, waiting for transfers between devices: none -> 232 us  [block_tick(): lax.all_gather(grads.astype(jnp.bfloat16), 'tok')]
    psum x2 -> x0, waiting for transfers between devices: 124 us -> none  [block_tick(): summed = lax.psum(grads.astype(jnp.bfloat16), 'tok').astype(jnp.float32)]
    reduce_sum x0 -> x2, other arithmetic: none -> 16.1 us  [block_tick(): jnp.sum(lax.all_gather(grads.astype(jnp.bfloat16), 'tok'), axis=0)]
where the time goes in v1:
time: 359 us; the launch traced here: 358 us
  waiting for transfers between devices  264 us (74%)
  other arithmetic  30.2 us (8%)
  matrix products  24.2 us (7%)
  between operations  15 us (4%)
  blocking collectives  11.3 us (3%)
  local copies, waits for them, and re-layouts  8.92 us (2%)
  starting transfers between devices  4.7 us (1%)
    all_gather x2, waiting for transfers between devices, block_tick(): lax.all_gather(grads.astype(jnp.bfloat16), 'tok')  232 us
    ppermute x1, waiting for transfers between devices, from_behind(): lax.ppermute(value, axis, [(source, source + steps) for source in range(f...  32.1 us
    reduce_sum x2, other arithmetic, block_tick(): jnp.sum(lax.all_gather(grads.astype(jnp.bfloat16), 'tok'), axis=0)  16.1 us
    psum x2, blocking collectives, block_tick(): total_sq = lax.psum(jnp.sum(summed * summed), 'head')  11.3 us
    dot_general x2, matrix products, apply_state(): lax.dot_general(mixed, state[2], contract, preferred_element_type=jnp.flo...  8.23 us
  transfers between devices with their start and end apart: 3, of which 3 were waited for; matrix products, arithmetic and copies ran while one was open for 1% of the time, Pallas kernels for 0%

profile of v1, /device:TPU:0, one launch (start us, length us, event | category | flops | bytes accessed | tf_op | source)
XLA Modules:
  0.0 358.5 jit_solution(18054076712388055410)
XLA Ops:
  6.5 1.6 copy.71
  11.0 1.3 fusion.63
  12.4 1.7 fusion.52
  16.7 119.5 %all-gather.5.cloned.1.call-done = bf16[16,3,256,512]{2,3,0,1:T(8,128)(2,1)} async-done(((bf16[2,3,256,512]{2,3,0,1:T(8,128)(2,1)}), bf16[16,3,256,512]{2,3,0,1:T(8,128)(2,1)}) %all-gather.5.cloned.1.call-update) | async-done | bytes 12582928 | tf_op jit(solution)/shard_map/all_gather | solution.py:52
  136.3 8.1 %reduce_sum.78 = bf16[2,3,256,512]{2,3,0,1:T(8,128)(2,1)} reduce(bf16[8,2,3,256,512]{3,4,1,0,2:T(8,128)(2,1)} %bitcast.234, bf16[]{:T(256)} %constant.7.clone.1), dimensions={0}, to_apply=%region_0.0 | reduce | flops 5505024 | bytes 14155778 | tf_op jit(solution)/shard_map/reduce_sum | solution.py:52
  144.3 1.8 copy.31
  146.2 1.4 fusion.1
  147.6 5.5 %psum.14 = f32[]{:T(128)} all-reduce(f32[]{:T(128)} %fusion.1), channel_id=1, replica_groups=mesh['ctx'=2,'tok'=8,'head'=2] {'head'}, use_global_device_ids=true, to_apply=%region_2.0 | all-reduce | flops 1 | bytes 8 | tf_op jit(solution)/shard_map/psum | solution.py:53
  154.7 1.8 divide_convert_fusion.1
  156.6 4.7 %collective-permute-start = (bf16[2,3,256,512]{3,2,0,1:T(8,128)(2,1)}, bf16[2,3,256,512]{3,2,0,1:T(8,128)(2,1)}, u32[]{:S(2)}, u32[]{:S(2)}) collective-permute-start(bf16[2,3,256,512]{3,2,0,1:T(8,128)(2,1)} %divide_convert_fusion.1), channel_id=1, source_target_pairs={{0,16},{1,17},{2,18},{3,19},{4,20},{5,21},{6,22},{7,23},{8,24},{9,... | collective-permute-start | bytes 4718600 | tf_op jit(solution)/shard_map/ppermute | solution.py:10
  161.2 32.1 %collective-permute-done = bf16[2,3,256,512]{3,2,0,1:T(8,128)(2,1)} collective-permute-done((bf16[2,3,256,512]{3,2,0,1:T(8,128)(2,1)}, bf16[2,3,256,512]{3,2,0,1:T(8,128)(2,1)}, u32[]{:S(2)}, u32[]{:S(2)}) %collective-permute-start) | collective-permute-done | bytes 1572896 | tf_op jit(solution)/shard_map/ppermute | solution.py:10
  193.3 1.6 copy_select_fusion
  197.5 1.3 fusion.60
  198.8 1.7 fusion.53
  201.8 1.3 maximum_bitcast_fusion.1
  203.8 3.3 fusion.74
  207.0 112.6 %all-gather.7.cloned.1.call-done = bf16[16,3,256,512]{2,3,0,1:T(8,128)(2,1)} async-done(((bf16[2,3,256,512]{2,3,0,1:T(8,128)(2,1)}), bf16[16,3,256,512]{2,3,0,1:T(8,128)(2,1)}) %all-gather.7.cloned.1.call-update) | async-done | bytes 12582928 | tf_op jit(solution)/shard_map/all_gather | solution.py:52
  319.7 8.1 %reduce_sum.82 = bf16[2,3,256,512]{2,3,0,1:T(8,128)(2,1)} reduce(bf16[8,2,3,256,512]{3,4,1,0,2:T(8,128)(2,1)} %bitcast.235, bf16[]{:T(256)} %constant.7.clone.1), dimensions={0}, to_apply=%region_5.6 | reduce | flops 5505024 | bytes 14155778 | tf_op jit(solution)/shard_map/reduce_sum | solution.py:52
  327.7 1.7 copy.43
  329.5 1.5 fusion.3
  330.9 4.6 %fusion.46 = bf16[1,2,768,256]{3,2,1,0:T(8,128)(2,1)} fusion(f32[2,512,768]{1,2,0:T(8,128)} %fusion.74, bf16[2,1,2,768,256]{4,3,2,1,0:T(8,128)(2,1)} %param.8, bf16[2,3,256,512]{3,2,0,1:T(8,128)(2,1)} %divide_convert_fusion.1), kind=kOutput, calls=%fused_computation.73 | convolution fusion | flops 810418176 | bytes 5767168 | tf_op jit(solution)/shard_map/vmap()/dot_general | solution.py:34
  335.5 5.8 %psum.15 = f32[]{:T(128)} all-reduce(f32[]{:T(128)} %fusion.3), channel_id=1, replica_groups=mesh['ctx'=2,'tok'=8,'head'=2] {'head'}, use_global_device_ids=true, to_apply=%region_7.8 | all-reduce | flops 1 | bytes 8 | tf_op jit(solution)/shard_map/psum | solution.py:53
  345.3 3.7 %fusion.47 = bf16[1,2,768,256]{3,2,1,0:T(8,128)(2,1)} fusion(f32[2,512,768]{1,2,0:T(8,128)S(1)} %fusion.64, bf16[2,1,2,768,256]{4,3,2,1,0:T(8,128)(2,1)} %param.8, bf16[2,3,256,512]{3,2,0,1:T(8,128)(2,1)} %copy-done.3), kind=kOutput, calls=%fused_computation.74 | convolution fusion | flops 810418176 | bytes 5767168 | tf_op jit(solution)/shard_map/vmap()/dot_general | solution.py:34
  349.0 2.7 maximum_bitcast_fusion.2
  (40 shorter events, 14.2 us)
Async XLA Ops:
  6.5 1.9 copy-start.1
  6.5 129.7 %all-gather.5.cloned.1.call-start = ((), (), s32[]{:S(2)}) async-start(), calls=%async_computation | async-start | bytes 14155776 | tf_op jit(solution)/shard_map/all_gather | solution.py:52
  9.0 0.7 copy-start.8
  9.0 1.4 copy-start.4
  16.7 303.0 %all-gather.7.cloned.1.call-start = ((), (), s32[]{:S(2)}) async-start(), calls=%async_computation.1 | async-start | bytes 14155776 | tf_op jit(solution)/shard_map/all_gather | solution.py:52
  144.3 9.5 %copy-start = (bf16[1,2,3,256,512]{4,3,2,1,0:T(8,128)(2,1)S(1)}, bf16[1,2,3,256,512]{4,3,2,1,0:T(8,128)(2,1)}, u32[]{:S(2)}) copy-start(bf16[1,2,3,256,512]{4,3,2,1,0:T(8,128)(2,1)} %param.10) | copy-start | bytes 4718596
  156.6 38.3 %copy-start.2 = (bf16[2,1,2,768,256]{4,3,2,1,0:T(8,128)(2,1)S(1)}, bf16[2,1,2,768,256]{4,3,2,1,0:T(8,128)(2,1)}, u32[]{:S(2)}) copy-start(bf16[2,1,2,768,256]{4,3,2,1,0:T(8,128)(2,1)} %param.6) | copy-start | bytes 4718596
  156.6 36.7 %collective-permute-start = (bf16[2,3,256,512]{3,2,0,1:T(8,128)(2,1)}, bf16[2,3,256,512]{3,2,0,1:T(8,128)(2,1)}, u32[]{:S(2)}, u32[]{:S(2)}) collective-permute-start(bf16[2,3,256,512]{3,2,0,1:T(8,128)(2,1)} %divide_convert_fusion.1), channel_id=1, source_target_pairs={{0,16},{1,17},{2,18},{3,19},{4,20},{5,21},{6,22},{7,23},{8,24},{9,... | collective-permute-start | bytes 4718600 | tf_op jit(solution)/shard_map/ppermute | solution.py:10
  195.4 1.4 copy-start.5
  201.8 2.0 copy-start.6
  342.9 1.9 copy-start.7
  343.6 1.1 copy-start.3
Sparse Core Ops, SparseCore 0:
  16.8 119.4 all-gather.4
  203.3 116.3 all-gather.6
